TPU v7x, 128 devices: a whole 4x4x4 slice. The times are simulated.
128 devices in a mesh: dp: 4 (over z), fsdp: 32 (over y, x, core).
Axes of the slice: x: 4, y: 4, z: 4, core: 2. Of those that a mesh axis runs over, the one named last changes fastest.
Arguments:
- logged: bfloat16 [2048, 8192], P('dp', 'fsdp'), may hold values from -6 to 6
- pairs: int32 [512, 2], P('dp'), may hold values from 0 to 511
- clicks: int32 [512], P('dp'), may hold values 0 or 1
- query_pairs: int32 [32, 2], P('dp'), may hold values from 0 to 511
- query_clicks: int32 [32], P('dp'), may hold values 0 or 1
- first_weight: bfloat16 [8192, 8192], P(None, 'fsdp'), may hold values from -0.0625 to 0.0625
- second_weight: bfloat16 [8192, 8192], P(None, 'fsdp'), may hold values from -0.0625 to 0.0625
- head_weight: float32 [8192], P('fsdp'), may hold values from -0.0625 to 0.0625
Outputs:
- solution: float32 [8192, 8192], P('dp', 'fsdp')
- influence: float32 [512], P('dp')
Inputs may be any that keep to these rules, and one draw needn't show every extreme that they name: Each block of 128 pairs indexes rows within the matching block of 512 logged rows. `query_pairs`: each block of 8 query pairs indexes rows within the matching block of 512 logged rows.
All inputs are finite; a program needn't handle non-finite values. No bound on the sum of `clicks` or of `query_clicks` on one device may be relied on, other than what follows from the above.
Results may differ from a plain program's by a relative error of at most 0.035.
Values may be sent and summed in bfloat16 or wider, within the bound.
A program may use at most 128 MiB of HBM per device.

v0:
```python
import jax
import jax.numpy as jnp
from jax import lax
from jax.sharding import PartitionSpec as P

DAMPING = 0.01


def pair_terms(first_score, second_score, outcome):
    signed = 2.0 * outcome.astype(jnp.float32) - 1.0
    margin = first_score - second_score
    slope_term = -signed * jax.nn.sigmoid(-signed * margin)
    curve_term = jax.nn.sigmoid(signed * margin) * jax.nn.sigmoid(-signed * margin)
    return (slope_term, curve_term)


def solver_total(value):
    return lax.psum(value, ("dp", "fsdp"))


def contract_rows(left, right):
    return lax.dot_general(
        left, right, (((0,), (0,)), ((), ())), preferred_element_type=jnp.float32
    )


def local(
    logged, pairs, clicks, query_pairs, query_clicks, first_weight, second_weight, head_weight
):
    npairs = pairs.shape[0]
    nqueries = query_pairs.shape[0]
    count = 2 * npairs
    row_ids = jnp.concatenate([pairs[:, 0], pairs[:, 1], query_pairs[:, 0], query_pairs[:, 1]])
    local_rows = jnp.take(logged, row_ids, axis=0)
    feats = lax.all_gather(local_rows, "fsdp", axis=1, tiled=True)
    hidden = jnp.tanh(jnp.dot(feats, first_weight, preferred_element_type=jnp.float32)).astype(
        jnp.bfloat16
    )
    second_pre = jnp.dot(
        lax.all_gather(hidden, "fsdp", axis=1, tiled=True),
        second_weight,
        preferred_element_type=jnp.float32,
    )
    output_act = jnp.tanh(second_pre)
    scores_all = lax.psum(jnp.sum(output_act * head_weight, axis=1), "fsdp")
    coef = (head_weight * (1.0 - output_act * output_act)).astype(jnp.bfloat16)
    back_term = lax.dot_general(
        coef, second_weight, (((1,), (1,)), ((), ())), preferred_element_type=jnp.float32
    )
    back = lax.psum_scatter(
        back_term.astype(jnp.bfloat16), "fsdp", scatter_dimension=1, tiled=True
    ).astype(jnp.float32)
    hidden_float = hidden.astype(jnp.float32)
    mixing = (1.0 - hidden_float * hidden_float) * back
    slope_train, curve_train = pair_terms(scores_all[:npairs], scores_all[npairs:count], clicks)
    slope_query = pair_terms(
        scores_all[count : count + nqueries], scores_all[count + nqueries :], query_clicks
    )[0]
    query_err = jnp.concatenate([slope_query, -slope_query])
    query_rows = (query_err[:, None] * mixing[count:]).astype(jnp.bfloat16)
    grad_local = contract_rows(feats[count:], query_rows)
    gradient = lax.psum_scatter(
        grad_local.astype(jnp.bfloat16), "dp", scatter_dimension=0, tiled=True
    ).astype(jnp.float32)
    train_feats = feats[:count]
    train_mix = mixing[:count]

    def apply_curvature(direction):
        packed = direction.astype(jnp.bfloat16)
        gathered = lax.all_gather(packed, "dp", axis=0, tiled=True)
        project = jnp.dot(train_feats, gathered, preferred_element_type=jnp.float32)
        response = lax.psum(jnp.sum(train_mix * project, axis=1), "fsdp")
        rdiff = response[:npairs] - response[npairs:]
        resp_err = jnp.concatenate([curve_train * rdiff, -curve_train * rdiff])
        resp_rows = (resp_err[:, None] * train_mix).astype(jnp.bfloat16)
        term = contract_rows(train_feats, resp_rows)
        return (packed, gathered, term, rdiff)

    norm_first = solver_total(jnp.sum(gradient * gradient))
    packed_first, gathered_first, local_first, rdiff_first = apply_curvature(gradient)
    product_first = lax.psum_scatter(
        local_first.astype(jnp.bfloat16), "dp", scatter_dimension=0, tiled=True
    ).astype(jnp.float32)
    curv_first = (
        solver_total(jnp.sum(packed_first.astype(jnp.float32) * product_first))
        + DAMPING * norm_first
    )
    alpha_first = norm_first / curv_first
    residual_next = gradient - alpha_first * (product_first + DAMPING * gradient)
    norm_next = solver_total(jnp.sum(residual_next * residual_next))
    direction_next = residual_next + norm_next / norm_first * gradient
    packed_next, gathered_next, local_next, rdiff_next = apply_curvature(direction_next)
    damped_part = DAMPING * jnp.sum(direction_next * direction_next)
    product_next = lax.psum_scatter(
        local_next.astype(jnp.bfloat16), "dp", scatter_dimension=0, tiled=True
    ).astype(jnp.float32)
    inner_part = jnp.sum(packed_next.astype(jnp.float32) * product_next) + damped_part
    curv_next = solver_total(inner_part)
    alpha_next = norm_next / curv_next
    solution = alpha_first * gradient + alpha_next * direction_next
    influence = -slope_train * (alpha_first * rdiff_first + alpha_next * rdiff_next)
    return (solution, influence)


def solution(mesh):
    placed = (
        P("dp", "fsdp"),
        P("dp", None),
        P("dp"),
        P("dp", None),
        P("dp"),
        P(None, "fsdp"),
        P(None, "fsdp"),
        P("fsdp"),
    )
    return jax.shard_map(
        local, mesh=mesh, in_specs=placed, out_specs=(P("dp", "fsdp"), P("dp")), check_vma=False
    )
```

profile of v0, /device:TPU:1, one launch (start us, length us, event | category | flops | bytes accessed | tf_op | source)
XLA Modules:
  0.0 815.9 jit_solution(4647815058639752397)
XLA Ops:
  7.2 0.0 all-gather.5.cloned.1.call-start
  7.2 0.8 slice_bitcast_fusion.3
  8.0 0.8 slice_bitcast_fusion.1
  8.7 0.1 fusion.33
  8.8 2.0 gather_fusion
  10.8 0.1 compare_and_fusion
  10.9 0.8 broadcast_select_fusion
  11.7 0.0 all-gather.5.cloned.1.call-update
  11.7 0.0 all-gather.7.cloned.1.call-start
  11.8 53.5 %all-gather.5.cloned.1.call-done = bf16[272,8192]{1,0:T(8,128)(2,1)} async-done(((bf16[272,256]{1,0:T(8,128)(2,1)}), bf16[272,8192]{1,0:T(8,128)(2,1)}) %all-gather.5.cloned.1.call-update) | async-done | bytes 4456464 | tf_op jit(solution)/shard_map/all_gather | solution.py:35
  65.2 5.5 fusion.17
  70.8 0.0 all-gather.7.cloned.1.call-update
  70.8 0.0 reduce-scatter.5.cloned.1.call-start
  70.8 49.4 %all-gather.7.cloned.1.call-done = bf16[272,8192]{1,0:T(8,128)(2,1)} async-done(((bf16[272,256]{1,0:T(8,128)(2,1)}), bf16[272,8192]{1,0:T(8,128)(2,1)}) %all-gather.7.cloned.1.call-update) | async-done | bytes 4456464 | tf_op jit(solution)/shard_map/all_gather | solution.py:40
  120.2 5.1 multiply_reduce_fusion.3
  125.4 3.5 convolution_convert_fusion
  128.8 0.0 reduce-scatter.5.cloned.1.call-update
  128.8 0.0 reduce-scatter.7.cloned.1.call-start
  128.9 62.7 %psum.49 = f32[272]{0:T(512)S(1)} all-reduce(f32[272]{0:T(512)S(1)} %get-tuple-element.23), channel_id=1, replica_groups=mesh['dp'=4,'fsdp'=32] {'fsdp'}, use_global_device_ids=true, to_apply=%region_1.2 | all-reduce | flops 272 | bytes 2176 | tf_op jit(solution)/shard_map/psum | solution.py:45
  191.6 0.1 fusion.37
  191.7 0.1 pad_maximum_fusion.2
  191.7 18.3 %reduce-scatter.5.cloned.1.call-done = bf16[272,256]{1,0:T(8,128)(2,1)} async-done(((bf16[272,8192]{1,0:T(8,128)(2,1)}), bf16[272,256]{1,0:T(8,128)(2,1)}) %reduce-scatter.5.cloned.1.call-update) | async-done | bytes 139280 | tf_op jit(solution)/shard_map/reduce_scatter | solution.py:50
  210.1 1.0 convert_multiply_fusion.5
  211.0 4.2 convolution_convert_fusion.3
  215.3 0.0 all-gather.9.cloned.1.call-start
  215.3 48.5 %reduce-scatter.7.cloned.1.call-done = bf16[2048,256]{1,0:T(8,128)(2,1)} async-done(((bf16[8192,256]{1,0:T(8,128)(2,1)}), bf16[2048,256]{1,0:T(8,128)(2,1)}) %reduce-scatter.7.cloned.1.call-update) | async-done | bytes 1048592 | tf_op jit(solution)/shard_map/reduce_scatter | solution.py:62
  263.9 0.0 reduce-scatter.9.cloned.1.call-start
  263.9 49.5 %all-gather.9.cloned.1.call-done = bf16[8192,256]{1,0:T(8,128)(2,1)} async-done(((bf16[2048,256]{1,0:T(8,128)(2,1)}), bf16[8192,256]{1,0:T(8,128)(2,1)}) %all-gather.9.cloned.1.call-update) | async-done | bytes 4194320 | tf_op jit(solution)/shard_map/all_gather | solution.py:70
  313.4 4.8 fusion.22
  318.2 62.7 %psum.51 = f32[256]{0:T(256)S(1)} all-reduce(f32[256]{0:T(256)S(1)} %fusion.22), channel_id=1, replica_groups=mesh['dp'=4,'fsdp'=32] {'fsdp'}, use_global_device_ids=true, to_apply=%region_7.8 | all-reduce | flops 256 | bytes 2048 | tf_op jit(solution)/shard_map/psum | solution.py:72
  380.9 5.5 convolution_convert_fusion.2
  386.5 0.0 all-gather.11.cloned.1.call-start
  386.5 46.8 %reduce-scatter.9.cloned.1.call-done = bf16[2048,256]{1,0:T(8,128)(2,1)} async-done(((bf16[8192,256]{1,0:T(8,128)(2,1)}), bf16[2048,256]{1,0:T(8,128)(2,1)}) %reduce-scatter.9.cloned.1.call-update) | async-done | bytes 1048592 | tf_op jit(solution)/shard_map/reduce_scatter | solution.py:81
  433.3 2.5 fusion.8
  435.8 64.6 %all-reduce = (f32[]{:T(128)}, f32[]{:T(128)}) all-reduce(f32[]{:T(128)} %get-tuple-element.3, f32[]{:T(128)} %get-tuple-element.2), channel_id=1, replica_groups=mesh['dp'=4,'fsdp'=32] {'dp','fsdp'}, use_global_device_ids=true, to_apply=%region_5.6 | all-reduce | flops 2 | bytes 16 | tf_op jit(solution)/shard_map/psum | solution.py:18
  502.3 2.4 multiply_reduce_fusion.2
  504.7 64.3 %psum.53 = f32[]{:T(128)} all-reduce(f32[]{:T(128)} %multiply_reduce_fusion.2), channel_id=1, replica_groups=mesh['dp'=4,'fsdp'=32] {'dp','fsdp'}, use_global_device_ids=true, to_apply=%region_12.13 | all-reduce | flops 1 | bytes 8 | tf_op jit(solution)/shard_map/psum | solution.py:18
  570.4 2.3 multiply_reduce_fusion
  572.7 0.0 reduce-scatter.11.cloned.1.call-start
  572.7 45.0 %all-gather.11.cloned.1.call-done = bf16[8192,256]{1,0:T(8,128)(2,1)} async-done(((bf16[2048,256]{1,0:T(8,128)(2,1)}), bf16[8192,256]{1,0:T(8,128)(2,1)}) %all-gather.11.cloned.1.call-update) | async-done | bytes 4194320 | tf_op jit(solution)/shard_map/all_gather | solution.py:70
  617.7 4.8 fusion.19
  622.5 62.7 %psum.54 = f32[256]{0:T(256)S(1)} all-reduce(f32[256]{0:T(256)S(1)} %fusion.19), channel_id=1, replica_groups=mesh['dp'=4,'fsdp'=32] {'fsdp'}, use_global_device_ids=true, to_apply=%region_14.15 | all-reduce | flops 256 | bytes 2048 | tf_op jit(solution)/shard_map/psum | solution.py:72
  685.2 5.5 convolution_convert_fusion.1
  691.5 46.1 %reduce-scatter.11.cloned.1.call-done = bf16[2048,256]{1,0:T(8,128)(2,1)} async-done(((bf16[8192,256]{1,0:T(8,128)(2,1)}), bf16[2048,256]{1,0:T(8,128)(2,1)}) %reduce-scatter.11.cloned.1.call-update) | async-done | bytes 1048592 | tf_op jit(solution)/shard_map/reduce_scatter | solution.py:94
  737.6 2.4 multiply_reduce_fusion.1
  740.6 64.5 %psum.55 = f32[]{:T(128)} all-reduce(f32[]{:T(128)S(6)} %add.83), channel_id=1, replica_groups=mesh['dp'=4,'fsdp'=32] {'dp','fsdp'}, use_global_device_ids=true, to_apply=%region_18.19 | all-reduce | flops 1 | bytes 8 | tf_op jit(solution)/shard_map/psum | solution.py:18
  806.5 0.5 add_multiply_fusion
  807.0 2.1 fusion.9
  (29 shorter events, 0.2 us)
Async XLA Ops:
  7.2 1.7 copy-start
  7.2 58.0 %all-gather.5.cloned.1.call-start = ((), (), s32[]{:S(2)}) async-start(), calls=%async_computation.4 | async-start | bytes 4595712 | tf_op jit(solution)/shard_map/all_gather | solution.py:35
  11.7 108.5 %copy-start.6 = (f32[256]{0:T(256)S(1)}, f32[256]{0:T(256)}, u32[]{:S(2)}) copy-start(f32[256]{0:T(256)} %param.15) | copy-start | bytes 3076
  11.7 108.5 %all-gather.7.cloned.1.call-start = ((), (), s32[]{:S(2)}) async-start(), calls=%async_computation.5 | async-start | bytes 4595712 | tf_op jit(solution)/shard_map/all_gather | solution.py:40
  70.8 139.3 %reduce-scatter.5.cloned.1.call-start = ((), (), s32[]{:S(2)}) async-start(), calls=%async_computation.6 | async-start | bytes 4595712 | tf_op jit(solution)/shard_map/reduce_scatter | solution.py:50
  120.2 5.1 copy-start.4
  128.8 62.8 %copy-start.8 = (s32[8]{0:T(128)S(1)}, s32[8]{0:T(128)}, u32[]{:S(2)}) copy-start(s32[8]{0:T(128)} %param.12) | copy-start | bytes 100
  128.8 81.3 %copy-start.5 = (bf16[272,256]{1,0:T(8,128)(2,1)S(1)}, bf16[272,256]{1,0:T(8,128)(2,1)}, u32[]{:S(2)}) copy-start(bf16[272,256]{1,0:T(8,128)(2,1)} %fusion.17) | copy-start | bytes 417796
  128.8 135.0 %reduce-scatter.7.cloned.1.call-start = ((), (), s32[]{:S(2)}) async-start(), calls=%async_computation.7 | async-start | bytes 5242880 | tf_op jit(solution)/shard_map/reduce_scatter | solution.py:62
  215.3 98.1 %all-gather.9.cloned.1.call-start = ((), (), s32[]{:S(2)}) async-start(), calls=%async_computation.8 | async-start | bytes 5242880 | tf_op jit(solution)/shard_map/all_gather | solution.py:70
  263.9 117.0 %copy-start.7 = (s32[128]{0:T(128)S(1)}, s32[128]{0:T(128)}, u32[]{:S(2)}) copy-start(s32[128]{0:T(128)} %param.10) | copy-start | bytes 1540
  263.9 169.4 %reduce-scatter.9.cloned.1.call-start = ((), (), s32[]{:S(2)}) async-start(), calls=%async_computation.9 | async-start | bytes 5242880 | tf_op jit(solution)/shard_map/reduce_scatter | solution.py:81
  386.4 46.9 %copy-start.1 = (bf16[2048,256]{1,0:T(8,128)(2,1)S(1)}, bf16[2048,256]{1,0:T(8,128)(2,1)}, u32[]{:S(2)}) copy-start(bf16[2048,256]{1,0:T(8,128)(2,1)} %reduce-scatter.7.cloned.1.call-done) | copy-start | bytes 3145732
  386.5 231.2 %all-gather.11.cloned.1.call-start = ((), (), s32[]{:S(2)}) async-start(), calls=%async_computation.10 | async-start | bytes 5242880 | tf_op jit(solution)/shard_map/all_gather | solution.py:70
  433.3 137.1 %copy-start.2 = (bf16[2048,256]{1,0:T(8,128)(2,1)S(1)}, bf16[2048,256]{1,0:T(8,128)(2,1)}, u32[]{:S(2)}) copy-start(bf16[2048,256]{1,0:T(8,128)(2,1)} %reduce-scatter.9.cloned.1.call-done) | copy-start | bytes 3145732
  572.7 164.9 %reduce-scatter.11.cloned.1.call-start = ((), (), s32[]{:S(2)}) async-start(), calls=%async_computation.11 | async-start | bytes 5242880 | tf_op jit(solution)/shard_map/reduce_scatter | solution.py:94
  690.7 46.9 %copy-start.3 = (bf16[2048,256]{1,0:T(8,128)(2,1)S(1)}, bf16[2048,256]{1,0:T(8,128)(2,1)}, u32[]{:S(2)}) copy-start(bf16[2048,256]{1,0:T(8,128)(2,1)} %get-tuple-element.12) | copy-start | bytes 3145732
Sparse Core Ops, SparseCore 0:
  11.8 53.3 all-gather.4
  70.9 49.2 all-gather.6
  129.0 81.0 reduce-scatter.4
  215.4 48.3 reduce-scatter.6
  265.4 47.9 all-gather.8
  386.6 46.6 reduce-scatter.8
  572.8 44.8 all-gather.10
  690.9 46.6 reduce-scatter.10
where the time goes:
time: 817 us; the launch traced here: 816 us
  blocking collectives  381 us (47%)
  waiting for transfers between devices  357 us (44%)
  matrix products  38.9 us (5%)
  between operations  20.2 us (2%)
  other arithmetic  14.2 us (2%)
    psum x3, blocking collectives, solver_total(): return lax.psum(value, ('dp', 'fsdp'))  193 us
    psum x2, blocking collectives, apply_curvature(): response = lax.psum(jnp.sum(train_mix * project, axis=1), 'fsdp')  125 us
    all_gather x2, waiting for transfers between devices, apply_curvature(): gathered = lax.all_gather(packed, 'dp', axis=0, tiled=True)  94.4 us
    psum x1, blocking collectives, local(): scores_all = lax.psum(jnp.sum(output_act * head_weight, axis=1), 'fsdp')  62.7 us
    all_gather x1, waiting for transfers between devices, local(): feats = lax.all_gather(local_rows, 'fsdp', axis=1, tiled=True)  53.5 us
    all_gather x1, waiting for transfers between devices, local(): lax.all_gather(hidden, 'fsdp', axis=1, tiled=True)  49.4 us
    reduce_scatter x1, waiting for transfers between devices, local(): lax.psum_scatter(grad_local.astype(jnp.bfloat16), 'dp', scatter_dimension...  48.5 us
    reduce_scatter x1, waiting for transfers between devices, local(): lax.psum_scatter(local_first.astype(jnp.bfloat16), 'dp', scatter_dimensio...  46.8 us
  transfers between devices with their start and end apart: 8, of which 8 were waited for; matrix products, arithmetic and copies ran while one was open for 0% of the time, Pallas kernels for 0%

commit v1 on v0

--- a/solution.py
+++ b/solution.py
@@ -15,7 +15,7 @@
 
 
 def solver_total(value):
-    return lax.psum(value, ("dp", "fsdp"))
+    return lax.psum(lax.psum(value, "fsdp"), axis_name="dp")
 
 
 def contract_rows(left, right):

time: 817 us -> 846 us (1.035)
  blocking collectives: 381 us -> 406 us
    psum x3 -> x6, blocking collectives: 193 us -> 218 us  [solver_total(): return lax.psum(lax.psum(value, 'fsdp'), axis_name='dp')]
where the time goes in v1:
time: 846 us; the launch traced here: 840 us
  blocking collectives  406 us (48%)
  waiting for transfers between devices  357 us (42%)
  matrix products  38.9 us (5%)
  between operations  20.2 us (2%)
  other arithmetic  14.2 us (2%)
    psum x6, blocking collectives, solver_total(): return lax.psum(lax.psum(value, 'fsdp'), axis_name='dp')  218 us
    psum x2, blocking collectives, apply_curvature(): response = lax.psum(jnp.sum(train_mix * project, axis=1), 'fsdp')  125 us
    all_gather x2, waiting for transfers between devices, apply_curvature(): gathered = lax.all_gather(packed, 'dp', axis=0, tiled=True)  94 us
    psum x1, blocking collectives, local(): scores_all = lax.psum(jnp.sum(output_act * head_weight, axis=1), 'fsdp')  62.7 us
    all_gather x1, waiting for transfers between devices, local(): feats = lax.all_gather(local_rows, 'fsdp', axis=1, tiled=True)  53.5 us
    all_gather x1, waiting for transfers between devices, local(): lax.all_gather(hidden, 'fsdp', axis=1, tiled=True)  49.4 us
    reduce_scatter x1, waiting for transfers between devices, local(): lax.psum_scatter(grad_local.astype(jnp.bfloat16), 'dp', scatter_dimension...  48.5 us
    reduce_scatter x1, waiting for transfers between devices, local(): lax.psum_scatter(local_first.astype(jnp.bfloat16), 'dp', scatter_dimensio...  46.8 us
  transfers between devices with their start and end apart: 8, of which 8 were waited for; matrix products, arithmetic and copies ran while one was open for 0% of the time, Pallas kernels for 0%

profile of v1, /device:TPU:1, one launch (start us, length us, event | category | flops | bytes accessed | tf_op | source)
XLA Modules:
  0.0 840.0 jit_solution(17097973850317161130)
XLA Ops:
  7.2 0.0 all-gather.5.cloned.1.call-start
  7.2 0.8 slice_bitcast_fusion.3
  8.0 0.8 slice_bitcast_fusion.1
  8.7 0.1 fusion.33
  8.8 2.0 gather_fusion
  10.8 0.1 compare_and_fusion
  10.9 0.8 broadcast_select_fusion
  11.7 0.0 all-gather.7.cloned.1.call-start
  11.8 53.5 %all-gather.5.cloned.1.call-done = bf16[272,8192]{1,0:T(8,128)(2,1)} async-done(((bf16[272,256]{1,0:T(8,128)(2,1)}), bf16[272,8192]{1,0:T(8,128)(2,1)}) %all-gather.5.cloned.1.call-update) | async-done | bytes 4456464 | tf_op jit(solution)/shard_map/all_gather | solution.py:35
  65.2 5.5 fusion.17
  70.8 0.0 reduce-scatter.5.cloned.1.call-start
  70.8 49.4 %all-gather.7.cloned.1.call-done = bf16[272,8192]{1,0:T(8,128)(2,1)} async-done(((bf16[272,256]{1,0:T(8,128)(2,1)}), bf16[272,8192]{1,0:T(8,128)(2,1)}) %all-gather.7.cloned.1.call-update) | async-done | bytes 4456464 | tf_op jit(solution)/shard_map/all_gather | solution.py:40
  120.2 5.1 multiply_reduce_fusion.3
  125.4 3.5 convolution_convert_fusion
  128.8 0.0 reduce-scatter.7.cloned.1.call-start
  128.9 62.7 %psum.77 = f32[272]{0:T(512)S(1)} all-reduce(f32[272]{0:T(512)S(1)} %get-tuple-element.25), channel_id=1, replica_groups=mesh['dp'=4,'fsdp'=32] {'fsdp'}, use_global_device_ids=true, to_apply=%region_1.2 | all-reduce | flops 272 | bytes 2176 | tf_op jit(solution)/shard_map/psum | solution.py:45
  191.6 0.1 fusion.37
  191.7 0.1 pad_maximum_fusion.2
  191.7 18.3 %reduce-scatter.5.cloned.1.call-done = bf16[272,256]{1,0:T(8,128)(2,1)} async-done(((bf16[272,8192]{1,0:T(8,128)(2,1)}), bf16[272,256]{1,0:T(8,128)(2,1)}) %reduce-scatter.5.cloned.1.call-update) | async-done | bytes 139280 | tf_op jit(solution)/shard_map/reduce_scatter | solution.py:50
  210.1 1.0 convert_multiply_fusion.5
  211.0 4.2 convolution_convert_fusion.3
  215.3 0.0 all-gather.9.cloned.1.call-start
  215.3 48.5 %reduce-scatter.7.cloned.1.call-done = bf16[2048,256]{1,0:T(8,128)(2,1)} async-done(((bf16[8192,256]{1,0:T(8,128)(2,1)}), bf16[2048,256]{1,0:T(8,128)(2,1)}) %reduce-scatter.7.cloned.1.call-update) | async-done | bytes 1048592 | tf_op jit(solution)/shard_map/reduce_scatter | solution.py:62
  263.9 0.0 reduce-scatter.9.cloned.1.call-start
  263.9 49.5 %all-gather.9.cloned.1.call-done = bf16[8192,256]{1,0:T(8,128)(2,1)} async-done(((bf16[2048,256]{1,0:T(8,128)(2,1)}), bf16[8192,256]{1,0:T(8,128)(2,1)}) %all-gather.9.cloned.1.call-update) | async-done | bytes 4194320 | tf_op jit(solution)/shard_map/all_gather | solution.py:70
  313.4 4.8 fusion.22
  318.2 62.7 %psum.80 = f32[256]{0:T(256)S(1)} all-reduce(f32[256]{0:T(256)S(1)} %fusion.22), channel_id=1, replica_groups=mesh['dp'=4,'fsdp'=32] {'fsdp'}, use_global_device_ids=true, to_apply=%region_8.9 | all-reduce | flops 256 | bytes 2048 | tf_op jit(solution)/shard_map/psum | solution.py:72
  380.9 5.5 convolution_convert_fusion.2
  386.5 0.0 all-gather.11.cloned.1.call-start
  386.5 46.8 %reduce-scatter.9.cloned.1.call-done = bf16[2048,256]{1,0:T(8,128)(2,1)} async-done(((bf16[8192,256]{1,0:T(8,128)(2,1)}), bf16[2048,256]{1,0:T(8,128)(2,1)}) %reduce-scatter.9.cloned.1.call-update) | async-done | bytes 1048592 | tf_op jit(solution)/shard_map/reduce_scatter | solution.py:81
  433.3 2.5 fusion.8
  435.8 63.3 %all-reduce = (f32[]{:T(128)}, f32[]{:T(128)}) all-reduce(f32[]{:T(128)} %get-tuple-element.3, f32[]{:T(128)} %get-tuple-element.2), channel_id=1, replica_groups=mesh['dp'=4,'fsdp'=32] {'fsdp'}, use_global_device_ids=true, to_apply=%region_5.6 | all-reduce | flops 2 | bytes 16 | tf_op jit(solution)/shard_map/psum | solution.py:18
  499.0 7.1 all-reduce.1
  508.1 2.4 multiply_reduce_fusion.2
  510.4 69.7 %psum.83 = f32[]{:T(128)} all-reduce(f32[]{:T(128)} %multiply_reduce_fusion.2), channel_id=1, replica_groups=mesh['dp'=4,'fsdp'=32] {'fsdp'}, use_global_device_ids=true, to_apply=%region_14.15 | all-reduce | flops 1 | bytes 8 | tf_op jit(solution)/shard_map/psum | solution.py:18
  580.1 7.6 psum.84
  589.0 2.3 multiply_reduce_fusion
  591.4 0.2 reduce-scatter.11.cloned.1.call-start
  591.6 44.5 %all-gather.11.cloned.1.call-done = bf16[8192,256]{1,0:T(8,128)(2,1)} async-done(((bf16[2048,256]{1,0:T(8,128)(2,1)}), bf16[8192,256]{1,0:T(8,128)(2,1)}) %all-gather.11.cloned.1.call-update) | async-done | bytes 4194320 | tf_op jit(solution)/shard_map/all_gather | solution.py:70
  636.1 4.8 fusion.19
  640.9 62.7 %psum.85 = f32[256]{0:T(256)S(1)} all-reduce(f32[256]{0:T(256)S(1)} %fusion.19), channel_id=1, replica_groups=mesh['dp'=4,'fsdp'=32] {'fsdp'}, use_global_device_ids=true, to_apply=%region_17.18 | all-reduce | flops 256 | bytes 2048 | tf_op jit(solution)/shard_map/psum | solution.py:72
  703.6 5.5 convolution_convert_fusion.1
  709.9 46.1 %reduce-scatter.11.cloned.1.call-done = bf16[2048,256]{1,0:T(8,128)(2,1)} async-done(((bf16[8192,256]{1,0:T(8,128)(2,1)}), bf16[2048,256]{1,0:T(8,128)(2,1)}) %reduce-scatter.11.cloned.1.call-update) | async-done | bytes 1048592 | tf_op jit(solution)/shard_map/reduce_scatter | solution.py:94
  756.0 2.4 multiply_reduce_fusion.1
  759.0 63.2 %psum.86 = f32[]{:T(128)} all-reduce(f32[]{:T(128)S(6)} %add.91), channel_id=1, replica_groups=mesh['dp'=4,'fsdp'=32] {'fsdp'}, use_global_device_ids=true, to_apply=%region_21.22 | all-reduce | flops 1 | bytes 8 | tf_op jit(solution)/shard_map/psum | solution.py:18
  822.2 7.1 psum.87
  830.6 0.5 add_multiply_fusion
  831.1 2.1 fusion.9
  (32 shorter events, 0.2 us)
Async XLA Ops:
  7.2 1.7 copy-start
  7.2 58.0 %all-gather.5.cloned.1.call-start = ((), (), s32[]{:S(2)}) async-start(), calls=%async_computation.4 | async-start | bytes 4595712 | tf_op jit(solution)/shard_map/all_gather | solution.py:35
  11.7 108.5 %copy-start.6 = (f32[256]{0:T(256)S(1)}, f32[256]{0:T(256)}, u32[]{:S(2)}) copy-start(f32[256]{0:T(256)} %param.15) | copy-start | bytes 3076
  11.7 108.5 %all-gather.7.cloned.1.call-start = ((), (), s32[]{:S(2)}) async-start(), calls=%async_computation.5 | async-start | bytes 4595712 | tf_op jit(solution)/shard_map/all_gather | solution.py:40
  70.8 139.3 %reduce-scatter.5.cloned.1.call-start = ((), (), s32[]{:S(2)}) async-start(), calls=%async_computation.6 | async-start | bytes 4595712 | tf_op jit(solution)/shard_map/reduce_scatter | solution.py:50
  120.2 5.1 copy-start.4
  128.8 62.8 %copy-start.8 = (s32[8]{0:T(128)S(1)}, s32[8]{0:T(128)}, u32[]{:S(2)}) copy-start(s32[8]{0:T(128)} %param.12) | copy-start | bytes 100
  128.8 81.3 %copy-start.5 = (bf16[272,256]{1,0:T(8,128)(2,1)S(1)}, bf16[272,256]{1,0:T(8,128)(2,1)}, u32[]{:S(2)}) copy-start(bf16[272,256]{1,0:T(8,128)(2,1)} %fusion.17) | copy-start | bytes 417796
  128.8 135.0 %reduce-scatter.7.cloned.1.call-start = ((), (), s32[]{:S(2)}) async-start(), calls=%async_computation.7 | async-start | bytes 5242880 | tf_op jit(solution)/shard_map/reduce_scatter | solution.py:62
  215.3 98.1 %all-gather.9.cloned.1.call-start = ((), (), s32[]{:S(2)}) async-start(), calls=%async_computation.8 | async-start | bytes 5242880 | tf_op jit(solution)/shard_map/all_gather | solution.py:70
  263.9 117.0 %copy-start.7 = (s32[128]{0:T(128)S(1)}, s32[128]{0:T(128)}, u32[]{:S(2)}) copy-start(s32[128]{0:T(128)} %param.10) | copy-start | bytes 1540
  263.9 169.4 %reduce-scatter.9.cloned.1.call-start = ((), (), s32[]{:S(2)}) async-start(), calls=%async_computation.9 | async-start | bytes 5242880 | tf_op jit(solution)/shard_map/reduce_scatter | solution.py:81
  386.4 46.9 %copy-start.1 = (bf16[2048,256]{1,0:T(8,128)(2,1)S(1)}, bf16[2048,256]{1,0:T(8,128)(2,1)}, u32[]{:S(2)}) copy-start(bf16[2048,256]{1,0:T(8,128)(2,1)} %reduce-scatter.7.cloned.1.call-done) | copy-start | bytes 3145732
  386.5 249.6 %all-gather.11.cloned.1.call-start = ((), (), s32[]{:S(2)}) async-start(), calls=%async_computation.10 | async-start | bytes 5242880 | tf_op jit(solution)/shard_map/all_gather | solution.py:70
  433.3 155.7 %copy-start.2 = (bf16[2048,256]{1,0:T(8,128)(2,1)S(1)}, bf16[2048,256]{1,0:T(8,128)(2,1)}, u32[]{:S(2)}) copy-start(bf16[2048,256]{1,0:T(8,128)(2,1)} %reduce-scatter.9.cloned.1.call-done) | copy-start | bytes 3145732
  591.4 164.6 %reduce-scatter.11.cloned.1.call-start = ((), (), s32[]{:S(2)}) async-start(), calls=%async_computation.11 | async-start | bytes 5242880 | tf_op jit(solution)/shard_map/reduce_scatter | solution.py:94
  709.1 46.8 %copy-start.3 = (bf16[2048,256]{1,0:T(8,128)(2,1)S(1)}, bf16[2048,256]{1,0:T(8,128)(2,1)}, u32[]{:S(2)}) copy-start(bf16[2048,256]{1,0:T(8,128)(2,1)} %get-tuple-element.14) | copy-start | bytes 3145732
Sparse Core Ops, SparseCore 0:
  11.8 53.3 all-gather.4
  70.9 49.2 all-gather.6
  129.0 81.0 reduce-scatter.4
  215.4 48.3 reduce-scatter.6
  265.4 47.9 all-gather.8
  386.6 46.6 reduce-scatter.8
  591.5 44.5 all-gather.10
  709.3 46.6 reduce-scatter.10
